TPU v7x, 32 devices: a whole 2x2x4 slice. The times are simulated.
32 devices in a mesh: row: 4 (over x, core), col: 8 (over z, y).
Axes of the slice: x: 2, y: 2, z: 4, core: 2. Of those that a mesh axis runs over, the one named last changes fastest.
Arguments:
- amplitudes: bfloat16 [4, 1024, 1024], P(None, 'row', 'col'), may hold values from -6 to 6
- factors: bfloat16 [3072, 65536], P('col', 'row'), may hold values from -0.029907227 to 0.029907227
- tile_mask: int32 [16, 16], replicated, may hold values 0 or 1
- tile_irrep: int32 [16], replicated, may hold values from 0 to 1
Outputs:
- residual: float32 [4, 64, 64], P(None, 'row', 'col')
All inputs are finite; a program needn't handle non-finite values.
Results may differ from a plain program's by a relative error of at most 0.007.
Values may be sent and summed in bfloat16 or wider, within the bound.
No kernel may reach another device: no remote copies, remote signals or barrier semaphores. Data moves between devices by JAX's collectives and lax.ppermute only.
A program may use at most 128 MiB of HBM per device.

v0:
```python
import functools

import jax
import jax.numpy as jnp
from jax import lax
from jax.experimental import pallas as pl
from jax.experimental.pallas import tpu as pltpu
from jax.sharding import PartitionSpec as P

TILE = 64
WIN = 64
LANES = 2 * WIN
BLOCK = 256


def chunk_sizes(total):
    middle = (total - 32) // 2
    if middle >= 16 and total % 16 == 0:
        return [8, middle, middle, 16, 8]
    return [total]


def group_of(count):
    for size in (8, 4, 2):
        if count % size == 0:
            return size
    return 1


def deinterleave(length, transposed=False):
    half = length // 2
    source = lax.broadcasted_iota(jnp.int32, (length, length), 1 if transposed else 0)
    target = lax.broadcasted_iota(jnp.int32, (length, length), 0 if transposed else 1)
    return (source % 2 * half + source // 2 == target).astype(jnp.float32).astype(jnp.bfloat16)


def relative(values, row):
    count = values.shape[0]
    bit = 1
    while bit < count:
        pairs = values.reshape((count // (2 * bit), 2, bit) + values.shape[1:])
        values = jnp.where(row & bit != 0, pairs[:, ::-1], pairs).reshape(values.shape)
        bit *= 2
    return values


def split_kernel(row_ref, *refs):
    half = len(refs) // 2
    for source, target in zip(refs[:half], refs[half:]):
        target[...] = source[...].reshape(target.shape)


def split_chunk(factors, row, start, count, row_count):
    flat = factors.shape[1]
    height = flat // LANES
    step = 8
    if count % step:
        return [
            lax.dynamic_slice_in_dim(factors, start * row_count + (row ^ x) * count, count, 0).reshape(
                count, height, LANES
            )
            for x in range(row_count)
        ]
    base = start * row_count // step

    def source_map(x, i, row_ref):
        return base + (row_ref[0] ^ x) * (count // step) + i, 0

    return pl.pallas_call(
        split_kernel,
        grid_spec=pltpu.PrefetchScalarGridSpec(
            num_scalar_prefetch=1,
            grid=(count // step,),
            in_specs=[pl.BlockSpec((step, flat), functools.partial(source_map, x)) for x in range(row_count)],
            out_specs=[pl.BlockSpec((step, height, LANES), lambda i, row_ref: (i, 0, 0))] * row_count,
        ),
        out_shape=[jax.ShapeDtypeStruct((count, height, LANES), factors.dtype)] * row_count,
        compiler_params=pltpu.CompilerParams(vmem_limit_bytes=16 << 20),
        cost_estimate=pl.CostEstimate(
            flops=0, bytes_accessed=4 * count * row_count * flat, transcendentals=0
        ),
    )(row[None], *([pltpu.with_memory_space_constraint(factors, pltpu.HBM)] * row_count))


def ladder_kernel(*refs, rows, group, plane_count):
    b_refs, (t_ref, acc_ref, o_ref, lhs, xs) = refs[:rows], refs[rows:]
    half = rows * b_refs[0].shape[1]

    @pl.when(pl.program_id(0) == 0)
    def _():
        o_ref[...] = acc_ref[...]

    def rows_of(q):
        return jnp.concatenate([b_ref[q] for b_ref in b_refs], 0)

    for q in range(group):
        b_q = rows_of(q)
        for j in range(half // LANES):
            turned = b_q[j * LANES : (j + 1) * LANES].T
            here = slice(q * WIN, (q + 1) * WIN)
            lhs[here, 2 * j * LANES : (2 * j + 1) * LANES] = turned[:WIN]
            lhs[here, (2 * j + 1) * LANES : (2 * j + 2) * LANES] = turned[WIN:]
    low = lax.broadcasted_iota(jnp.int32, (LANES, LANES), 1) < WIN
    for block in range(half // LANES):
        columns = slice(block * BLOCK, (block + 1) * BLOCK)
        for plane in range(plane_count):
            depth = 2 * half if plane == plane_count - 1 else (block + 1) * BLOCK
            x = jnp.dot(
                lhs[:, :depth], t_ref[plane, :depth, columns], preferred_element_type=jnp.float32
            ).astype(jnp.bfloat16)
            for q in range(group):
                xs[q, plane * WIN : (plane + 1) * WIN, :] = x[q * WIN : (q + 1) * WIN]
        for q in range(group):
            piece = rows_of(q)[block * LANES : (block + 1) * LANES]
            zero = jnp.zeros_like(piece)
            both = jnp.concatenate([jnp.where(low, piece, zero), jnp.where(low, zero, piece)], 0)
            o_ref[...] += jnp.dot(xs[q], both, preferred_element_type=jnp.float32)


def contract(acc, pieces, planes):
    rows = len(pieces)
    count, height, _ = pieces[0].shape
    plane_count, width, _ = planes.shape
    group = group_of(count)
    return pl.pallas_call(
        functools.partial(ladder_kernel, rows=rows, group=group, plane_count=plane_count),
        grid=(count // group,),
        in_specs=[pl.BlockSpec((group, height, LANES), lambda i: (i, 0, 0))] * rows
        + [pl.BlockSpec(memory_space=pltpu.VMEM)]
        + [pl.BlockSpec(acc.shape, lambda i: (0, 0))],
        out_specs=pl.BlockSpec(acc.shape, lambda i: (0, 0)),
        out_shape=jax.ShapeDtypeStruct(acc.shape, jnp.float32),
        scratch_shapes=[
            pltpu.VMEM((group * WIN, width), jnp.bfloat16),
            pltpu.VMEM((group, plane_count * WIN, BLOCK), jnp.bfloat16),
        ],
        compiler_params=pltpu.CompilerParams(vmem_limit_bytes=24 << 20),
        cost_estimate=pl.CostEstimate(
            flops=2 * count * plane_count * WIN * width * width,
            bytes_accessed=2 * count * width * WIN,
            transcendentals=0,
        ),
    )(*pieces, planes, acc)


def ring_gather(piece, axis, size):
    order = list(range(0, size, 2)) + list(range(1, size, 2))[::-1]
    ahead = [(order[i], order[(i + 1) % size]) for i in range(size)]
    behind = [(b, a) for a, b in ahead]
    me = lax.axis_index(axis)
    place = jnp.where(me % 2 == 0, me // 2, size - 1 - me // 2)
    height, width = piece.shape
    half = height // 2
    whole = jnp.zeros((height, size * width), piece.dtype)

    def put(whole, part, top, step):
        at = (place + step) % size
        owner = jnp.where(2 * at < size, 2 * at, 2 * size - 1 - 2 * at)
        return lax.dynamic_update_slice(whole, part, (top, owner * width))

    up, down = piece[:half], piece[half:]
    whole = put(whole, piece, 0, 0)
    for step in range(1, size):
        up = lax.ppermute(up, axis, ahead)
        down = lax.ppermute(down, axis, behind)
        whole = put(whole, up, 0, size - step)
        whole = put(whole, down, half, step)
    return whole


def pack_kernel(at_ref, mask_ref, irrep_ref, t_ref, o_ref, *, turned):
    _, c_here, d_here = t_ref.shape
    c_tiles, d_tiles = c_here // TILE, d_here // TILE
    lane_tile = lax.broadcasted_iota(jnp.int32, (TILE, d_here), 1) // TILE
    planes = [[], []]
    for ct in range(c_tiles):
        c_tile = at_ref[0] * c_tiles + ct
        keep = jnp.zeros((TILE, d_here), jnp.int32)
        cross = jnp.zeros((TILE, d_here), jnp.int32)
        for dt in range(d_tiles):
            d_tile = at_ref[1] * d_tiles + dt
            keep = jnp.where(lane_tile == dt, mask_ref[c_tile, d_tile], keep)
            cross = jnp.where(lane_tile == dt, irrep_ref[c_tile] ^ irrep_ref[d_tile], cross)
        t = [t_ref[p, ct * TILE : (ct + 1) * TILE].astype(jnp.float32) for p in range(4)]
        for plane, (first, second) in zip(planes, ((t[0], t[1]), (t[3], t[2]))):
            chosen = jnp.where(cross == 0, first, second)
            plane.append(jnp.where(keep != 0, chosen, 0.0).astype(jnp.bfloat16))
    for s, plane in enumerate(planes):
        value = jnp.concatenate(plane, 0)
        if turned:
            value = jnp.dot(deinterleave(BLOCK, True), value, preferred_element_type=jnp.float32).astype(jnp.bfloat16)
            value = jnp.dot(value, deinterleave(d_here), preferred_element_type=jnp.float32).astype(jnp.bfloat16)
        for r in range(s, o_ref.shape[0], 2):
            o_ref[r] = value


def fits(c_here, d_here):
    return c_here == BLOCK and d_here == LANES


def pack(amplitudes, tile_mask, tile_irrep, row, col, row_count):
    _, c_here, d_here = amplitudes.shape
    return pl.pallas_call(
        functools.partial(pack_kernel, turned=fits(c_here, d_here)),
        in_specs=[pl.BlockSpec(memory_space=pltpu.SMEM)] * 3 + [pl.BlockSpec(memory_space=pltpu.VMEM)],
        out_specs=pl.BlockSpec(memory_space=pltpu.VMEM),
        out_shape=jax.ShapeDtypeStruct((row_count, c_here, d_here), jnp.bfloat16),
        compiler_params=pltpu.CompilerParams(vmem_limit_bytes=8 << 20),
        cost_estimate=pl.CostEstimate(flops=1 << 24, bytes_accessed=amplitudes.size * 2, transcendentals=0),
    )(jnp.stack([row, col]), tile_mask, tile_irrep, amplitudes)


def expand_kernel(row_ref, irrep_ref, own_ref, other_ref, o_ref):
    row = row_ref[0]
    count = own_ref.shape[0] // BLOCK
    tiles = BLOCK // TILE
    even = row % 2 == 0
    low = lax.broadcasted_iota(jnp.int32, (BLOCK, LANES), 1) < WIN

    def at(block):
        return pl.ds(pl.multiple_of(block * BLOCK, BLOCK), BLOCK)

    def planes(i, j):
        def ordered(ref):
            value = ref[at(i ^ row), at(j ^ row)].astype(jnp.float32)
            first, second = value[:, :LANES], value[:, LANES:]
            return jnp.concatenate(
                [
                    jnp.where(low, first, pltpu.roll(second, WIN, 1)),
                    jnp.where(low, pltpu.roll(first, WIN, 1), second),
                ],
                1,
            )

        own, other = ordered(own_ref), ordered(other_ref)
        return jnp.where(even, own, other), jnp.where(even, other, own)

    def irreps(block, axis):
        tile = lax.broadcasted_iota(jnp.int32, (BLOCK, BLOCK), axis) % LANES // (TILE // 2)
        value = jnp.zeros((BLOCK, BLOCK), jnp.int32)
        for t in range(tiles):
            value = jnp.where(tile == t, irrep_ref[(block ^ row) * tiles + t], value)
        return value

    def put(plane, i, j, value):
        o_ref[plane, at(i), at(j)] = value.astype(jnp.bfloat16)

    @pl.loop(0, count)
    def _(i):
        same = irreps(i, 0) == irreps(i, 1)
        a, b = planes(i, i)
        put(0, i, i, jnp.where(same, a, 0.0))
        put(1, i, i, jnp.where(same, b, 0.0))
        put(2, i, i, jnp.where(same, 0.0, a + b.T))

        @pl.loop(i + 1, count)
        def _(j):
            same = irreps(i, 0) == irreps(j, 1)
            a_up, b_up = planes(i, j)
            a_down, b_down = planes(j, i)
            b_turned = b_down.T
            put(0, i, j, jnp.where(same, a_up + a_down.T, 0.0))
            put(1, i, j, jnp.where(same, b_up + b_turned, 0.0))
            put(2, i, j, jnp.where(same, 0.0, a_up + b_turned))
            same = irreps(j, 0) == irreps(i, 1)
            put(2, j, i, jnp.where(same, 0.0, a_down + b_up.T))


def expand(own, other, tile_irrep, row):
    vmem = pl.BlockSpec(memory_space=pltpu.VMEM)
    return pl.pallas_call(
        expand_kernel,
        in_specs=[pl.BlockSpec(memory_space=pltpu.SMEM)] * 2 + [vmem] * 2,
        out_specs=vmem,
        out_shape=jax.ShapeDtypeStruct((3, *own.shape), own.dtype),
        compiler_params=pltpu.CompilerParams(vmem_limit_bytes=12 << 20),
        cost_estimate=pl.CostEstimate(flops=1 << 24, bytes_accessed=own.size * 10, transcendentals=0),
    )(row[None], tile_irrep, own, other)


def expand_small(own, other, tile_irrep, row, row_count):
    size = own.shape[0]
    c_here = size // row_count
    even = row % 2 == 0

    def by_row(plane):
        moved = relative(plane.reshape(row_count, c_here, size), row).reshape(size // BLOCK, BLOCK, size)
        return jnp.einsum(
            "xc,jcd->jxd", deinterleave(BLOCK, True), moved, preferred_element_type=jnp.float32
        ).reshape(size, size)

    def ordered(plane):
        return by_row(by_row(plane).astype(plane.dtype).T).T

    own, other = ordered(own), ordered(other)
    a, b = jnp.where(even, own, other), jnp.where(even, other, own)
    irrep = relative(tile_irrep.reshape(row_count, c_here // TILE), row)
    order = jnp.broadcast_to(
        irrep.reshape(-1, 1, BLOCK // TILE, 1), (size // BLOCK, 2, BLOCK // TILE, TILE // 2)
    ).reshape(size)
    same = order[:, None] == order[None, :]
    block = jnp.arange(size, dtype=jnp.int32) // BLOCK
    above, level = block[:, None] < block[None, :], block[:, None] == block[None, :]

    def upper(plane):
        chosen = jnp.where(level, plane, jnp.where(above, plane + plane.T, 0.0))
        return jnp.where(same, chosen, 0.0)

    return jnp.stack([upper(a), upper(b), jnp.where(same, 0.0, a + b.T)]).astype(jnp.bfloat16)


def amplitude_planes(amplitudes, tile_mask, tile_irrep, row, col, row_count, col_count):
    _, c_here, d_here = amplitudes.shape
    to_send = pack(amplitudes, tile_mask, tile_irrep, row, col, row_count)
    mine = lax.all_to_all(to_send, "row", 0, 0)
    own = ring_gather(mine.reshape(c_here * row_count, d_here), "col", col_count)
    other = lax.ppermute(own, "row", [(i, i ^ 1) for i in range(row_count)])
    if fits(c_here, d_here):
        return expand(own, other, tile_irrep, row)
    return expand_small(own, other, tile_irrep, row, row_count)


def per_device(amplitudes, factors, tile_mask, tile_irrep, *, row_count, col_count):
    pair_count = amplitudes.shape[0]
    row, col = lax.axis_index("row"), lax.axis_index("col")
    acc = jnp.zeros((3 * WIN, LANES), jnp.float32)
    chunks = []
    start = 0
    for count in chunk_sizes(factors.shape[0] // row_count):
        pieces = split_chunk(factors, row, start, count, row_count)
        arrived = [pieces[0]]
        for x in range(1, row_count):
            arrived.append(lax.ppermute(pieces[x], "row", [(i, i ^ x) for i in range(row_count)]))
        chunks.append(arrived)
        start += count
    planes = amplitude_planes(amplitudes, tile_mask, tile_irrep, row, col, row_count, col_count)
    for chunk in chunks:
        acc = contract(acc, chunk, planes)
    upper = (acc[:, :WIN] + acc[:, WIN:]).reshape(3, WIN, WIN)
    turned = upper.transpose(0, 2, 1)
    flipped = jnp.stack([upper[0] + turned[0], turned[2], upper[2], upper[1] + turned[1]])
    a_count, b_count = WIN // row_count, WIN // col_count
    blocks = flipped.reshape(pair_count, col_count, b_count, row_count, a_count).transpose(3, 1, 0, 2, 4)
    blocks = blocks.reshape(row_count * col_count, pair_count * b_count * a_count)
    summed = lax.all_to_all(blocks, ("row", "col"), 0, 0, tiled=True).sum(0)
    return summed.reshape(pair_count, b_count, a_count).transpose(0, 2, 1)


def solution(mesh):
    row_count, col_count = mesh.shape["row"], mesh.shape["col"]
    return jax.shard_map(
        functools.partial(per_device, row_count=row_count, col_count=col_count),
        mesh=mesh,
        in_specs=(P(None, "row", "col"), P("col", "row"), P(), P()),
        out_specs=P(None, "row", "col"),
        check_vma=False,
    )
```

profile of v0, /device:TPU:0, one launch (start us, length us, event | category | flops | bytes accessed | tf_op | source)
XLA Modules:
  0.0 214.7 jit_solution(16287739676509310897)
XLA Ops:
  2.4 1.2 shard_map.47
  3.6 10.0 %all_to_all.15 = bf16[4,256,128]{2,1,0:T(8,128)(2,1)S(1)} all-to-all(bf16[4,256,128]{2,1,0:T(8,128)(2,1)S(1)} %shard_map.47), channel_id=1, replica_groups=mesh['row'=4,'col'=8] {'row'}, dimensions={0} | all-to-all | bytes 524288 | tf_op jit(solution)/shard_map/all_to_all | solution.py:315
  13.6 1.6 collective-permute-start.3
  16.1 2.6 %collective-permute-done.3 = bf16[512,128]{1,0:T(8,128)(2,1)S(1)} collective-permute-done((bf16[512,128]{1,0:T(8,128)(2,1)S(1)}, bf16[512,128]{1,0:T(8,128)(2,1)S(1)}, u32[]{:S(2)}, u32[]{:S(2)}) %collective-permute-start.3) | collective-permute-done | bytes 131104 | tf_op jit(solution)/shard_map/ppermute | solution.py:164
  18.7 1.6 collective-permute-start.5
  20.8 3.1 %collective-permute-done.5 = bf16[512,128]{1,0:T(8,128)(2,1)S(1)} collective-permute-done((bf16[512,128]{1,0:T(8,128)(2,1)S(1)}, bf16[512,128]{1,0:T(8,128)(2,1)S(1)}, u32[]{:S(2)}, u32[]{:S(2)}) %collective-permute-start.5) | collective-permute-done | bytes 131104 | tf_op jit(solution)/shard_map/ppermute | solution.py:164
  23.9 1.6 collective-permute-start.7
  26.0 3.9 %collective-permute-done.7 = bf16[512,128]{1,0:T(8,128)(2,1)S(1)} collective-permute-done((bf16[512,128]{1,0:T(8,128)(2,1)S(1)}, bf16[512,128]{1,0:T(8,128)(2,1)S(1)}, u32[]{:S(2)}, u32[]{:S(2)}) %collective-permute-start.7) | collective-permute-done | bytes 131104 | tf_op jit(solution)/shard_map/ppermute | solution.py:164
  29.9 1.6 collective-permute-start.9
  32.3 3.4 %collective-permute-done.9 = bf16[512,128]{1,0:T(8,128)(2,1)S(1)} collective-permute-done((bf16[512,128]{1,0:T(8,128)(2,1)S(1)}, bf16[512,128]{1,0:T(8,128)(2,1)S(1)}, u32[]{:S(2)}, u32[]{:S(2)}) %collective-permute-start.9) | collective-permute-done | bytes 131104 | tf_op jit(solution)/shard_map/ppermute | solution.py:164
  35.8 1.6 collective-permute-start.11
  37.9 2.9 %collective-permute-done.11 = bf16[512,128]{1,0:T(8,128)(2,1)S(1)} collective-permute-done((bf16[512,128]{1,0:T(8,128)(2,1)S(1)}, bf16[512,128]{1,0:T(8,128)(2,1)S(1)}, u32[]{:S(2)}, u32[]{:S(2)}) %collective-permute-start.11) | collective-permute-done | bytes 131104 | tf_op jit(solution)/shard_map/ppermute | solution.py:164
  40.7 1.6 collective-permute-start.13
  42.9 2.8 %collective-permute-done.13 = bf16[512,128]{1,0:T(8,128)(2,1)S(1)} collective-permute-done((bf16[512,128]{1,0:T(8,128)(2,1)S(1)}, bf16[512,128]{1,0:T(8,128)(2,1)S(1)}, u32[]{:S(2)}, u32[]{:S(2)}) %collective-permute-start.13) | collective-permute-done | bytes 131104 | tf_op jit(solution)/shard_map/ppermute | solution.py:164
  45.7 1.6 collective-permute-start.15
  47.9 2.8 %collective-permute-done.15 = bf16[512,128]{1,0:T(8,128)(2,1)S(1)} collective-permute-done((bf16[512,128]{1,0:T(8,128)(2,1)S(1)}, bf16[512,128]{1,0:T(8,128)(2,1)S(1)}, u32[]{:S(2)}, u32[]{:S(2)}) %collective-permute-start.15) | collective-permute-done | bytes 131104 | tf_op jit(solution)/shard_map/ppermute | solution.py:164
  50.7 1.6 collective-permute-done.16
  52.5 3.8 %shard_map.51 = (bf16[32,128,128]{2,1,0:T(8,128)(2,1)S(1)}, bf16[32,128,128]{2,1,0:T(8,128)(2,1)S(1)}, bf16[32,128,128]{2,1,0:T(8,128)(2,1)S(1)}, bf16[32,128,128]{2,1,0:T(8,128)(2,1)S(1)}) custom-call(s32[1]{0:T(128)} %bitcast.row_ref, bf16[384,16384]{1,0:T(8,128)(2,1)} %refs_3_.9, bf16[384,16384]{1,0:T(8,128)(2,1)} %refs_3_.9, bf16[384,16384]{1,0:T(8,128)(2,1)} %refs_3_.9, ...), custom_call_target="tpu_custom_call" | custom-call | bytes 8388608 | tf_op jit(solution)/shard_map/pallas_call | solution.py:69
  58.2 1.5 shard_map.52
  63.3 3.6 %shard_map.50 = (bf16[32,128,128]{2,1,0:T(8,128)(2,1)S(1)}, bf16[32,128,128]{2,1,0:T(8,128)(2,1)S(1)}, bf16[32,128,128]{2,1,0:T(8,128)(2,1)S(1)}, bf16[32,128,128]{2,1,0:T(8,128)(2,1)S(1)}) custom-call(s32[1]{0:T(128)} %bitcast.row_ref, bf16[384,16384]{1,0:T(8,128)(2,1)} %refs_3_.9, bf16[384,16384]{1,0:T(8,128)(2,1)} %refs_3_.9, bf16[384,16384]{1,0:T(8,128)(2,1)} %refs_3_.9, ...), custom_call_target="tpu_custom_call" | custom-call | bytes 8388608 | tf_op jit(solution)/shard_map/pallas_call | solution.py:69
  66.9 2.0 shard_map.49
  68.9 1.5 shard_map.46
  70.5 4.2 %shard_map.48.refs_4_ = bf16[3,1024,1024]{2,1,0:T(8,128)(2,1)S(1)} custom-call(s32[1]{0:T(128)} %bitcast.row_ref, s32[16]{0:T(128)S(1)} %copy-done.3, bf16[1024,1024]{1,0:T(8,128)(2,1)S(1)} %constant_dynamic-update-slice_fusion.own_ref, bf16[1024,1024]{1,0:T(8,128)(2,1)S(1)} %collective-permute-done.17.other_ref), custom_call_target="tpu_custom_call" | custom-call | flops 16777216 | bytes 10485760 | tf_op jit(solution)/shard_map/pallas_call | solution.py:271
  74.7 36.1 %collective-permute-done.28.refs_2_ = bf16[8,128,128]{2,1,0:T(8,128)(2,1)S(1)} collective-permute-done((bf16[8,128,128]{2,1,0:T(8,128)(2,1)S(1)}, bf16[8,128,128]{2,1,0:T(8,128)(2,1)S(1)}, u32[]{:S(2)}, u32[]{:S(2)}) %collective-permute-start.28) | collective-permute-done | bytes 262176 | tf_op jit(solution)/shard_map/ppermute | solution.py:333
  110.8 4.1 %collective-permute-done.29.refs_3_ = bf16[8,128,128]{2,1,0:T(8,128)(2,1)S(1)} collective-permute-done((bf16[8,128,128]{2,1,0:T(8,128)(2,1)S(1)}, bf16[8,128,128]{2,1,0:T(8,128)(2,1)S(1)}, u32[]{:S(2)}, u32[]{:S(2)}) %collective-permute-start.29) | collective-permute-done | bytes 262176 | tf_op jit(solution)/shard_map/ppermute | solution.py:333
  115.9 5.2 %shard_map.53.refs_5_ = f32[192,128]{1,0:T(8,128)S(1)} custom-call(bf16[8,128,128]{2,1,0:T(8,128)(2,1)S(1)} %get-tuple-element.41.refs_0_, bf16[8,128,128]{2,1,0:T(8,128)(2,1)S(1)} %collective-permute-done.27.refs_1_, bf16[8,128,128]{2,1,0:T(8,128)(2,1)S(1)} %collective-permute-done.28.refs_2_, bf16[8,128,128]{2,1,0:T(8,128)(2,1)S(1)} %collective-permute-done.29.refs_3_, ...), custom_call_target="tpu_custom_call" | custom-call | flops 3221225472 | bytes 1048576 | tf_op jit(solution)/shard_map/pallas_call | solution.py:125
  123.3 20.9 %shard_map.54.refs_5_ = f32[192,128]{1,0:T(8,128)S(1)} custom-call(bf16[32,128,128]{2,1,0:T(8,128)(2,1)S(1)} %get-tuple-element.37.refs_0_, bf16[32,128,128]{2,1,0:T(8,128)(2,1)S(1)} %collective-permute-done.24.refs_1_, bf16[32,128,128]{2,1,0:T(8,128)(2,1)S(1)} %collective-permute-done.25.refs_2_, bf16[32,128,128]{2,1,0:T(8,128)(2,1)S(1)} %collective-permute-done.26.refs_3_, ...), custom_call_target="tpu_custom_call" | custom-call | flops 12884901888 | bytes 4194304 | tf_op jit(solution)/shard_map/pallas_call | solution.py:125
  145.5 17.1 %collective-permute-done.23.refs_3_ = bf16[32,128,128]{2,1,0:T(8,128)(2,1)S(1)} collective-permute-done((bf16[32,128,128]{2,1,0:T(8,128)(2,1)S(1)}, bf16[32,128,128]{2,1,0:T(8,128)(2,1)S(1)}, u32[]{:S(2)}, u32[]{:S(2)}) %collective-permute-start.23) | collective-permute-done | bytes 1048608 | tf_op jit(solution)/shard_map/ppermute | solution.py:333
  163.6 20.9 %shard_map.55.refs_5_ = f32[192,128]{1,0:T(8,128)S(1)} custom-call(bf16[32,128,128]{2,1,0:T(8,128)(2,1)S(1)} %get-tuple-element.33.refs_0_, bf16[32,128,128]{2,1,0:T(8,128)(2,1)S(1)} %collective-permute-done.21.refs_1_, bf16[32,128,128]{2,1,0:T(8,128)(2,1)S(1)} %collective-permute-done.22.refs_2_, bf16[32,128,128]{2,1,0:T(8,128)(2,1)S(1)} %collective-permute-done.23.refs_3_, ...), custom_call_target="tpu_custom_call" | custom-call | flops 12884901888 | bytes 4194304 | tf_op jit(solution)/shard_map/pallas_call | solution.py:125
  185.6 10.7 %shard_map.56.refs_5_ = f32[192,128]{1,0:T(8,128)S(1)} custom-call(bf16[16,128,128]{2,1,0:T(8,128)(2,1)S(1)} %get-tuple-element.29.refs_0_, bf16[16,128,128]{2,1,0:T(8,128)(2,1)S(1)} %collective-permute-done.18.refs_1_, bf16[16,128,128]{2,1,0:T(8,128)(2,1)S(1)} %collective-permute-done.19.refs_2_, bf16[16,128,128]{2,1,0:T(8,128)(2,1)S(1)} %collective-permute-done.20.refs_3_, ...), custom_call_target="tpu_custom_call" | custom-call | flops 6442450944 | bytes 2097152 | tf_op jit(solution)/shard_map/pallas_call | solution.py:125
  196.3 5.2 %shard_map.57 = f32[192,128]{1,0:T(8,128)S(1)} custom-call(bf16[8,128,128]{2,1,0:T(8,128)(2,1)S(1)} %get-tuple-element.25.refs_0_, bf16[8,128,128]{2,1,0:T(8,128)(2,1)S(1)} %collective-permute-done.refs_1_, bf16[8,128,128]{2,1,0:T(8,128)(2,1)S(1)} %collective-permute-done.1.refs_2_, bf16[8,128,128]{2,1,0:T(8,128)(2,1)S(1)} %collective-permute-done.2.refs_3_, ...), custom_call_target="tpu_custom_call" | custom-call | flops 3221225472 | bytes 1048576 | tf_op jit(solution)/shard_map/pallas_call | solution.py:125
  202.6 11.3 %all_to_all.16 = f32[32,1,512]{2,1,0:T(1,128)S(1)} all-to-all(f32[32,1,512]{2,1,0:T(1,128)S(1)} %all_to_all.12), channel_id=1, replica_groups=mesh['row'=4,'col'=8] {'row','col'}, dimensions={0} | all-to-all | bytes 131072 | tf_op jit(solution)/shard_map/all_to_all | solution.py:345
  (85 shorter events, 20.6 us)
Async XLA Ops:
  0.1 0.9 copy-start
  13.6 5.0 %collective-permute-start.3 = (bf16[512,128]{1,0:T(8,128)(2,1)S(1)}, bf16[512,128]{1,0:T(8,128)(2,1)S(1)}, u32[]{:S(2)}, u32[]{:S(2)}) collective-permute-start(bf16[512,128]{1,0:T(8,128)(2,1)S(1)} %bitcast.24), channel_id=1, source_target_pairs={{0,2},{2,4},{4,6},{6,7},{7,5},{5,3},{3,1},{1,0},{8,10},{10,12},{12... | collective-permute-start | bytes 393224 | tf_op jit(solution)/shard_map/ppermute | solution.py:164
  15.3 5.0 %collective-permute-start.4 = (bf16[512,128]{1,0:T(8,128)(2,1)S(1)}, bf16[512,128]{1,0:T(8,128)(2,1)S(1)}, u32[]{:S(2)}, u32[]{:S(2)}) collective-permute-start(bf16[512,128]{1,0:T(8,128)(2,1)S(1)} %bitcast.23), channel_id=1, source_target_pairs={{2,0},{4,2},{6,4},{7,6},{5,7},{3,5},{1,3},{0,1},{10,8},{12,10},{14... | collective-permute-start | bytes 393224 | tf_op jit(solution)/shard_map/ppermute | solution.py:165
  18.7 5.2 %collective-permute-start.5 = (bf16[512,128]{1,0:T(8,128)(2,1)S(1)}, bf16[512,128]{1,0:T(8,128)(2,1)S(1)}, u32[]{:S(2)}, u32[]{:S(2)}) collective-permute-start(bf16[512,128]{1,0:T(8,128)(2,1)S(1)} %collective-permute-done.3), channel_id=1, source_target_pairs={{0,2},{2,4},{4,6},{6,7},{7,5},{5,3},{3,1},{1,0},{8,10},{10,12},{12... | collective-permute-start | bytes 393224 | tf_op jit(solution)/shard_map/ppermute | solution.py:164
  20.2 5.2 %collective-permute-start.6 = (bf16[512,128]{1,0:T(8,128)(2,1)S(1)}, bf16[512,128]{1,0:T(8,128)(2,1)S(1)}, u32[]{:S(2)}, u32[]{:S(2)}) collective-permute-start(bf16[512,128]{1,0:T(8,128)(2,1)S(1)} %collective-permute-done.4), channel_id=1, source_target_pairs={{2,0},{4,2},{6,4},{7,6},{5,7},{3,5},{1,3},{0,1},{10,8},{12,10},{14... | collective-permute-start | bytes 393224 | tf_op jit(solution)/shard_map/ppermute | solution.py:165
  23.9 6.0 %collective-permute-start.7 = (bf16[512,128]{1,0:T(8,128)(2,1)S(1)}, bf16[512,128]{1,0:T(8,128)(2,1)S(1)}, u32[]{:S(2)}, u32[]{:S(2)}) collective-permute-start(bf16[512,128]{1,0:T(8,128)(2,1)S(1)} %collective-permute-done.5), channel_id=1, source_target_pairs={{0,2},{2,4},{4,6},{6,7},{7,5},{5,3},{3,1},{1,0},{8,10},{10,12},{12... | collective-permute-start | bytes 393224 | tf_op jit(solution)/shard_map/ppermute | solution.py:164
  25.4 6.3 %collective-permute-start.8 = (bf16[512,128]{1,0:T(8,128)(2,1)S(1)}, bf16[512,128]{1,0:T(8,128)(2,1)S(1)}, u32[]{:S(2)}, u32[]{:S(2)}) collective-permute-start(bf16[512,128]{1,0:T(8,128)(2,1)S(1)} %collective-permute-done.6), channel_id=1, source_target_pairs={{2,0},{4,2},{6,4},{7,6},{5,7},{3,5},{1,3},{0,1},{10,8},{12,10},{14... | collective-permute-start | bytes 393224 | tf_op jit(solution)/shard_map/ppermute | solution.py:165
  29.9 5.8 %collective-permute-start.9 = (bf16[512,128]{1,0:T(8,128)(2,1)S(1)}, bf16[512,128]{1,0:T(8,128)(2,1)S(1)}, u32[]{:S(2)}, u32[]{:S(2)}) collective-permute-start(bf16[512,128]{1,0:T(8,128)(2,1)S(1)} %collective-permute-done.7), channel_id=1, source_target_pairs={{0,2},{2,4},{4,6},{6,7},{7,5},{5,3},{3,1},{1,0},{8,10},{10,12},{12... | collective-permute-start | bytes 393224 | tf_op jit(solution)/shard_map/ppermute | solution.py:164
  31.7 5.6 %collective-permute-start.10 = (bf16[512,128]{1,0:T(8,128)(2,1)S(1)}, bf16[512,128]{1,0:T(8,128)(2,1)S(1)}, u32[]{:S(2)}, u32[]{:S(2)}) collective-permute-start(bf16[512,128]{1,0:T(8,128)(2,1)S(1)} %collective-permute-done.8), channel_id=1, source_target_pairs={{2,0},{4,2},{6,4},{7,6},{5,7},{3,5},{1,3},{0,1},{10,8},{12,10},{14... | collective-permute-start | bytes 393224 | tf_op jit(solution)/shard_map/ppermute | solution.py:165
  35.8 5.0 %collective-permute-start.11 = (bf16[512,128]{1,0:T(8,128)(2,1)S(1)}, bf16[512,128]{1,0:T(8,128)(2,1)S(1)}, u32[]{:S(2)}, u32[]{:S(2)}) collective-permute-start(bf16[512,128]{1,0:T(8,128)(2,1)S(1)} %collective-permute-done.9), channel_id=1, source_target_pairs={{0,2},{2,4},{4,6},{6,7},{7,5},{5,3},{3,1},{1,0},{8,10},{10,12},{12... | collective-permute-start | bytes 393224 | tf_op jit(solution)/shard_map/ppermute | solution.py:164
  37.3 5.0 %collective-permute-start.12 = (bf16[512,128]{1,0:T(8,128)(2,1)S(1)}, bf16[512,128]{1,0:T(8,128)(2,1)S(1)}, u32[]{:S(2)}, u32[]{:S(2)}) collective-permute-start(bf16[512,128]{1,0:T(8,128)(2,1)S(1)} %collective-permute-done.10), channel_id=1, source_target_pairs={{2,0},{4,2},{6,4},{7,6},{5,7},{3,5},{1,3},{0,1},{10,8},{12,10},{14... | collective-permute-start | bytes 393224 | tf_op jit(solution)/shard_map/ppermute | solution.py:165
  40.7 5.0 %collective-permute-start.13 = (bf16[512,128]{1,0:T(8,128)(2,1)S(1)}, bf16[512,128]{1,0:T(8,128)(2,1)S(1)}, u32[]{:S(2)}, u32[]{:S(2)}) collective-permute-start(bf16[512,128]{1,0:T(8,128)(2,1)S(1)} %collective-permute-done.11), channel_id=1, source_target_pairs={{0,2},{2,4},{4,6},{6,7},{7,5},{5,3},{3,1},{1,0},{8,10},{10,12},{12... | collective-permute-start | bytes 393224 | tf_op jit(solution)/shard_map/ppermute | solution.py:164
  42.4 5.0 %collective-permute-start.14 = (bf16[512,128]{1,0:T(8,128)(2,1)S(1)}, bf16[512,128]{1,0:T(8,128)(2,1)S(1)}, u32[]{:S(2)}, u32[]{:S(2)}) collective-permute-start(bf16[512,128]{1,0:T(8,128)(2,1)S(1)} %collective-permute-done.12), channel_id=1, source_target_pairs={{2,0},{4,2},{6,4},{7,6},{5,7},{3,5},{1,3},{0,1},{10,8},{12,10},{14... | collective-permute-start | bytes 393224 | tf_op jit(solution)/shard_map/ppermute | solution.py:165
  45.7 5.0 %collective-permute-start.15 = (bf16[512,128]{1,0:T(8,128)(2,1)S(1)}, bf16[512,128]{1,0:T(8,128)(2,1)S(1)}, u32[]{:S(2)}, u32[]{:S(2)}) collective-permute-start(bf16[512,128]{1,0:T(8,128)(2,1)S(1)} %collective-permute-done.13), channel_id=1, source_target_pairs={{0,2},{2,4},{4,6},{6,7},{7,5},{5,3},{3,1},{1,0},{8,10},{10,12},{12... | collective-permute-start | bytes 393224 | tf_op jit(solution)/shard_map/ppermute | solution.py:164
  47.4 5.0 %collective-permute-start.16 = (bf16[512,128]{1,0:T(8,128)(2,1)S(1)}, bf16[512,128]{1,0:T(8,128)(2,1)S(1)}, u32[]{:S(2)}, u32[]{:S(2)}) collective-permute-start(bf16[512,128]{1,0:T(8,128)(2,1)S(1)} %collective-permute-done.14), channel_id=1, source_target_pairs={{2,0},{4,2},{6,4},{7,6},{5,7},{3,5},{1,3},{0,1},{10,8},{12,10},{14... | collective-permute-start | bytes 393224 | tf_op jit(solution)/shard_map/ppermute | solution.py:165
  52.4 10.1 %collective-permute-start.17 = (bf16[1024,1024]{1,0:T(8,128)(2,1)S(1)}, bf16[1024,1024]{1,0:T(8,128)(2,1)S(1)}, u32[]{:S(2)}, u32[]{:S(2)}) collective-permute-start(bf16[1024,1024]{1,0:T(8,128)(2,1)S(1)} %constant_dynamic-update-slice_fusion.own_ref), channel_id=1, source_target_pairs={{0,8},{8,0},{16,24},{24,16},{1,9},{9,1},{17,25},{25,17},{2,10},{10... | collective-permute-start | bytes 6291464 | tf_op jit(solution)/shard_map/ppermute | solution.py:317
  56.3 64.8 %collective-permute-start.24 = (bf16[32,128,128]{2,1,0:T(8,128)(2,1)S(1)}, bf16[32,128,128]{2,1,0:T(8,128)(2,1)S(1)}, u32[]{:S(2)}, u32[]{:S(2)}) collective-permute-start(bf16[32,128,128]{2,1,0:T(8,128)(2,1)S(1)} %get-tuple-element.38), channel_id=1, source_target_pairs={{0,8},{8,0},{16,24},{24,16},{1,9},{9,1},{17,25},{25,17},{2,10},{10... | collective-permute-start | bytes 3145736 | tf_op jit(solution)/shard_map/ppermute | solution.py:333
  56.7 65.5 %collective-permute-start.25 = (bf16[32,128,128]{2,1,0:T(8,128)(2,1)S(1)}, bf16[32,128,128]{2,1,0:T(8,128)(2,1)S(1)}, u32[]{:S(2)}, u32[]{:S(2)}) collective-permute-start(bf16[32,128,128]{2,1,0:T(8,128)(2,1)S(1)} %get-tuple-element.39), channel_id=1, source_target_pairs={{0,16},{8,24},{16,0},{24,8},{1,17},{9,25},{17,1},{25,9},{2,18},{10... | collective-permute-start | bytes 3145736 | tf_op jit(solution)/shard_map/ppermute | solution.py:333
  57.6 64.7 %collective-permute-start.26 = (bf16[32,128,128]{2,1,0:T(8,128)(2,1)S(1)}, bf16[32,128,128]{2,1,0:T(8,128)(2,1)S(1)}, u32[]{:S(2)}, u32[]{:S(2)}) collective-permute-start(bf16[32,128,128]{2,1,0:T(8,128)(2,1)S(1)} %get-tuple-element.40), channel_id=1, source_target_pairs={{0,24},{8,16},{16,8},{24,0},{1,25},{9,17},{17,9},{25,1},{2,26},{10... | collective-permute-start | bytes 3145736 | tf_op jit(solution)/shard_map/ppermute | solution.py:333
  59.8 1.8 collective-permute-start.27
  61.6 49.2 %collective-permute-start.28 = (bf16[8,128,128]{2,1,0:T(8,128)(2,1)S(1)}, bf16[8,128,128]{2,1,0:T(8,128)(2,1)S(1)}, u32[]{:S(2)}, u32[]{:S(2)}) collective-permute-start(bf16[8,128,128]{2,1,0:T(8,128)(2,1)S(1)} %get-tuple-element.43), channel_id=1, source_target_pairs={{0,16},{8,24},{16,0},{24,8},{1,17},{9,25},{17,1},{25,9},{2,18},{10... | collective-permute-start | bytes 786440 | tf_op jit(solution)/shard_map/ppermute | solution.py:333
  62.5 52.4 %collective-permute-start.29 = (bf16[8,128,128]{2,1,0:T(8,128)(2,1)S(1)}, bf16[8,128,128]{2,1,0:T(8,128)(2,1)S(1)}, u32[]{:S(2)}, u32[]{:S(2)}) collective-permute-start(bf16[8,128,128]{2,1,0:T(8,128)(2,1)S(1)} %get-tuple-element.44), channel_id=1, source_target_pairs={{0,24},{8,16},{16,8},{24,0},{1,25},{9,17},{17,9},{25,1},{2,26},{10... | collective-permute-start | bytes 786440 | tf_op jit(solution)/shard_map/ppermute | solution.py:333
  68.9 1.6 copy-start.3
  110.8 33.5 %collective-permute-start.21 = (bf16[32,128,128]{2,1,0:T(8,128)(2,1)S(1)}, bf16[32,128,128]{2,1,0:T(8,128)(2,1)S(1)}, u32[]{:S(2)}, u32[]{:S(2)}) collective-permute-start(bf16[32,128,128]{2,1,0:T(8,128)(2,1)S(1)} %get-tuple-element.34), channel_id=1, source_target_pairs={{0,8},{8,0},{16,24},{24,16},{1,9},{9,1},{17,25},{25,17},{2,10},{10... | collective-permute-start | bytes 3145736 | tf_op jit(solution)/shard_map/ppermute | solution.py:333
  114.9 30.1 %collective-permute-start.22 = (bf16[32,128,128]{2,1,0:T(8,128)(2,1)S(1)}, bf16[32,128,128]{2,1,0:T(8,128)(2,1)S(1)}, u32[]{:S(2)}, u32[]{:S(2)}) collective-permute-start(bf16[32,128,128]{2,1,0:T(8,128)(2,1)S(1)} %get-tuple-element.35), channel_id=1, source_target_pairs={{0,16},{8,24},{16,0},{24,8},{1,17},{9,25},{17,1},{25,9},{2,18},{10... | collective-permute-start | bytes 3145736 | tf_op jit(solution)/shard_map/ppermute | solution.py:333
  121.1 41.5 %collective-permute-start.23 = (bf16[32,128,128]{2,1,0:T(8,128)(2,1)S(1)}, bf16[32,128,128]{2,1,0:T(8,128)(2,1)S(1)}, u32[]{:S(2)}, u32[]{:S(2)}) collective-permute-start(bf16[32,128,128]{2,1,0:T(8,128)(2,1)S(1)} %get-tuple-element.36), channel_id=1, source_target_pairs={{0,24},{8,16},{16,8},{24,0},{1,25},{9,17},{17,9},{25,1},{2,26},{10... | collective-permute-start | bytes 3145736 | tf_op jit(solution)/shard_map/ppermute | solution.py:333
  122.1 62.3 %collective-permute-start.18 = (bf16[16,128,128]{2,1,0:T(8,128)(2,1)S(1)}, bf16[16,128,128]{2,1,0:T(8,128)(2,1)S(1)}, u32[]{:S(2)}, u32[]{:S(2)}) collective-permute-start(bf16[16,128,128]{2,1,0:T(8,128)(2,1)S(1)} %get-tuple-element.30), channel_id=1, source_target_pairs={{0,8},{8,0},{16,24},{24,16},{1,9},{9,1},{17,25},{25,17},{2,10},{10... | collective-permute-start | bytes 1572872 | tf_op jit(solution)/shard_map/ppermute | solution.py:333
  122.4 63.2 %collective-permute-start.19 = (bf16[16,128,128]{2,1,0:T(8,128)(2,1)S(1)}, bf16[16,128,128]{2,1,0:T(8,128)(2,1)S(1)}, u32[]{:S(2)}, u32[]{:S(2)}) collective-permute-start(bf16[16,128,128]{2,1,0:T(8,128)(2,1)S(1)} %get-tuple-element.31), channel_id=1, source_target_pairs={{0,16},{8,24},{16,0},{24,8},{1,17},{9,25},{17,1},{25,9},{2,18},{10... | collective-permute-start | bytes 1572872 | tf_op jit(solution)/shard_map/ppermute | solution.py:333
  144.3 41.3 %collective-permute-start.20 = (bf16[16,128,128]{2,1,0:T(8,128)(2,1)S(1)}, bf16[16,128,128]{2,1,0:T(8,128)(2,1)S(1)}, u32[]{:S(2)}, u32[]{:S(2)}) collective-permute-start(bf16[16,128,128]{2,1,0:T(8,128)(2,1)S(1)} %get-tuple-element.32), channel_id=1, source_target_pairs={{0,24},{8,16},{16,8},{24,0},{1,25},{9,17},{17,9},{25,1},{2,26},{10... | collective-permute-start | bytes 1572872 | tf_op jit(solution)/shard_map/ppermute | solution.py:333
  145.0 51.2 %collective-permute-start = (bf16[8,128,128]{2,1,0:T(8,128)(2,1)S(1)}, bf16[8,128,128]{2,1,0:T(8,128)(2,1)S(1)}, u32[]{:S(2)}, u32[]{:S(2)}) collective-permute-start(bf16[8,128,128]{2,1,0:T(8,128)(2,1)S(1)} %get-tuple-element.26), channel_id=1, source_target_pairs={{0,8},{8,0},{16,24},{24,16},{1,9},{9,1},{17,25},{25,17},{2,10},{10... | collective-permute-start | bytes 786440 | tf_op jit(solution)/shard_map/ppermute | solution.py:333
  162.6 33.7 %collective-permute-start.1 = (bf16[8,128,128]{2,1,0:T(8,128)(2,1)S(1)}, bf16[8,128,128]{2,1,0:T(8,128)(2,1)S(1)}, u32[]{:S(2)}, u32[]{:S(2)}) collective-permute-start(bf16[8,128,128]{2,1,0:T(8,128)(2,1)S(1)} %get-tuple-element.27), channel_id=1, source_target_pairs={{0,16},{8,24},{16,0},{24,8},{1,17},{9,25},{17,1},{25,9},{2,18},{10... | collective-permute-start | bytes 786440 | tf_op jit(solution)/shard_map/ppermute | solution.py:333
  184.5 11.8 %collective-permute-start.2 = (bf16[8,128,128]{2,1,0:T(8,128)(2,1)S(1)}, bf16[8,128,128]{2,1,0:T(8,128)(2,1)S(1)}, u32[]{:S(2)}, u32[]{:S(2)}) collective-permute-start(bf16[8,128,128]{2,1,0:T(8,128)(2,1)S(1)} %get-tuple-element.28), channel_id=1, source_target_pairs={{0,24},{8,16},{16,8},{24,0},{1,25},{9,17},{17,9},{25,1},{2,26},{10... | collective-permute-start | bytes 786440 | tf_op jit(solution)/shard_map/ppermute | solution.py:333
  (2 other events, 1.4 us)
where the time goes:
time: 215 us
  waiting for transfers between devices  81.9 us (38%)
  Pallas kernels  80.8 us (38%)
  starting transfers between devices  25.2 us (12%)
  blocking collectives  21.4 us (10%)
  local copies, waits for them, and re-layouts  4.71 us (2%)
    pallas_call x5, Pallas kernels, contract(): pl.pallas_call(functools.partial(ladder_kernel, rows=rows, group=group, p...  63 us
    ppermute x15, waiting for transfers between devices, per_device(): lax.ppermute(pieces[x], 'row', [(i, i ^ x) for i in range(row_count)])  58.5 us
    ppermute x7, waiting for transfers between devices, ring_gather(): up = lax.ppermute(up, axis, ahead)  21.5 us
    pallas_call x5, Pallas kernels, split_chunk(): pl.pallas_call(split_kernel, grid_spec=pltpu.PrefetchScalarGridSpec(num_s...  12.5 us
    all_to_all x1, blocking collectives, per_device(): summed = lax.all_to_all(blocks, ('row', 'col'), 0, 0, tiled=True).sum(0)  11.3 us
    ppermute x7, starting transfers between devices, ring_gather(): up = lax.ppermute(up, axis, ahead)  11.1 us
    ppermute x15, starting transfers between devices, per_device(): lax.ppermute(pieces[x], 'row', [(i, i ^ x) for i in range(row_count)])  10.7 us
    all_to_all x1, blocking collectives, amplitude_planes(): mine = lax.all_to_all(to_send, 'row', 0, 0)  10 us
  transfers between devices with their start and end apart: 30, of which 14 were waited for; matrix products, arithmetic and copies ran while one was open for 0% of the time, Pallas kernels for 35%

commit v1 on v0

--- a/solution.py
+++ b/solution.py
@@ -46,11 +46,13 @@
 
 def split_kernel(row_ref, *refs):
     half = len(refs) // 2
+    step = refs[0].shape[0]
+    here = pl.ds(pl.program_id(0) * step, step)
     for source, target in zip(refs[:half], refs[half:]):
-        target[...] = source[...].reshape(target.shape)
-
-
-def split_chunk(factors, row, start, count, row_count):
+        target[here] = source[...].reshape(step, *target.shape[1:])
+
+
+def split_chunk(factors, row, start, count, row_count, steps):
     flat = factors.shape[1]
     height = flat // LANES
     step = 8
@@ -59,7 +61,7 @@
             lax.dynamic_slice_in_dim(factors, start * row_count + (row ^ x) * count, count, 0).reshape(
                 count, height, LANES
             )
-            for x in range(row_count)
+            for x in steps
         ]
     base = start * row_count // step
 
@@ -71,70 +73,78 @@
         grid_spec=pltpu.PrefetchScalarGridSpec(
             num_scalar_prefetch=1,
             grid=(count // step,),
-            in_specs=[pl.BlockSpec((step, flat), functools.partial(source_map, x)) for x in range(row_count)],
-            out_specs=[pl.BlockSpec((step, height, LANES), lambda i, row_ref: (i, 0, 0))] * row_count,
+            in_specs=[pl.BlockSpec((step, flat), functools.partial(source_map, x)) for x in steps],
+            out_specs=[pl.BlockSpec(memory_space=pltpu.VMEM)] * len(steps),
         ),
-        out_shape=[jax.ShapeDtypeStruct((count, height, LANES), factors.dtype)] * row_count,
-        compiler_params=pltpu.CompilerParams(vmem_limit_bytes=16 << 20),
+        out_shape=[jax.ShapeDtypeStruct((count, height, LANES), factors.dtype)] * len(steps),
+        compiler_params=pltpu.CompilerParams(vmem_limit_bytes=8 << 20),
         cost_estimate=pl.CostEstimate(
-            flops=0, bytes_accessed=4 * count * row_count * flat, transcendentals=0
+            flops=0, bytes_accessed=4 * count * len(steps) * flat, transcendentals=0
         ),
-    )(row[None], *([pltpu.with_memory_space_constraint(factors, pltpu.HBM)] * row_count))
-
-
-def ladder_kernel(*refs, rows, group, plane_count):
-    b_refs, (t_ref, acc_ref, o_ref, lhs, xs) = refs[:rows], refs[rows:]
+    )(row[None], *([pltpu.with_memory_space_constraint(factors, pltpu.HBM)] * len(steps)))
+
+
+def ladder_kernel(*refs, rows, group, team, plane_count):
+    b_refs, (t_ref, acc_ref, o_ref, lhs, xs, rhs) = refs[:rows], refs[rows:]
     half = rows * b_refs[0].shape[1]
-
-    @pl.when(pl.program_id(0) == 0)
-    def _():
-        o_ref[...] = acc_ref[...]
-
-    def rows_of(q):
-        return jnp.concatenate([b_ref[q] for b_ref in b_refs], 0)
-
-    for q in range(group):
-        b_q = rows_of(q)
-        for j in range(half // LANES):
-            turned = b_q[j * LANES : (j + 1) * LANES].T
-            here = slice(q * WIN, (q + 1) * WIN)
-            lhs[here, 2 * j * LANES : (2 * j + 1) * LANES] = turned[:WIN]
-            lhs[here, (2 * j + 1) * LANES : (2 * j + 2) * LANES] = turned[WIN:]
-    low = lax.broadcasted_iota(jnp.int32, (LANES, LANES), 1) < WIN
-    for block in range(half // LANES):
-        columns = slice(block * BLOCK, (block + 1) * BLOCK)
-        for plane in range(plane_count):
-            depth = 2 * half if plane == plane_count - 1 else (block + 1) * BLOCK
-            x = jnp.dot(
-                lhs[:, :depth], t_ref[plane, :depth, columns], preferred_element_type=jnp.float32
-            ).astype(jnp.bfloat16)
-            for q in range(group):
-                xs[q, plane * WIN : (plane + 1) * WIN, :] = x[q * WIN : (q + 1) * WIN]
-        for q in range(group):
-            piece = rows_of(q)[block * LANES : (block + 1) * LANES]
-            zero = jnp.zeros_like(piece)
-            both = jnp.concatenate([jnp.where(low, piece, zero), jnp.where(low, zero, piece)], 0)
-            o_ref[...] += jnp.dot(xs[q], both, preferred_element_type=jnp.float32)
+    tall = plane_count * WIN
+    low = lax.broadcasted_iota(jnp.int32, (tall, LANES), 1) < WIN
+    o_ref[...] = acc_ref[...]
+
+    @pl.loop(0, b_refs[0].shape[0] // group)
+    def _(step):
+        b_all = [jnp.concatenate([b_ref[step * group + q] for b_ref in b_refs], 0) for q in range(group)]
+        for q, b_q in enumerate(b_all):
+            for j in range(half // LANES):
+                turned = b_q[j * LANES : (j + 1) * LANES].T
+                here = slice(q * WIN, (q + 1) * WIN)
+                lhs[here, 2 * j * LANES : (2 * j + 1) * LANES] = turned[:WIN]
+                lhs[here, (2 * j + 1) * LANES : (2 * j + 2) * LANES] = turned[WIN:]
+        for block in range(half // LANES):
+            columns = slice(block * BLOCK, (block + 1) * BLOCK)
+            for plane in range(plane_count):
+                depth = 2 * half if plane == plane_count - 1 else (block + 1) * BLOCK
+                x = jnp.dot(
+                    lhs[:, :depth], t_ref[plane, :depth, columns], preferred_element_type=jnp.float32
+                ).astype(jnp.bfloat16)
+                for q in range(group):
+                    top = q % team * tall + plane * WIN
+                    xs[q // team, top : top + WIN, columns] = x[q * WIN : (q + 1) * WIN]
+        for q in range(0, group, 2):
+            lanes = slice(q % team * WIN, (q % team + 2) * WIN)
+            for j in range(half // LANES):
+                first, second = (b_all[q + k][j * LANES : (j + 1) * LANES] for k in range(2))
+                rhs[q // team, 2 * j * LANES : (2 * j + 1) * LANES, lanes] = jnp.concatenate(
+                    [first[:, :WIN], second[:, :WIN]], 1
+                )
+                rhs[q // team, (2 * j + 1) * LANES : (2 * j + 2) * LANES, lanes] = jnp.concatenate(
+                    [first[:, WIN:], second[:, WIN:]], 1
+                )
+        for t in range(group // team):
+            y = jnp.dot(xs[t], rhs[t], preferred_element_type=jnp.float32)
+            for q in range(0, team, 2):
+                lanes = slice(q * WIN, (q + 2) * WIN)
+                o_ref[...] += jnp.where(low, y[q * tall : (q + 1) * tall, lanes], y[(q + 1) * tall : (q + 2) * tall, lanes])
 
 
 def contract(acc, pieces, planes):
     rows = len(pieces)
-    count, height, _ = pieces[0].shape
+    count = pieces[0].shape[0]
     plane_count, width, _ = planes.shape
     group = group_of(count)
+    team = min(group, 4)
+    vmem = pl.BlockSpec(memory_space=pltpu.VMEM)
     return pl.pallas_call(
-        functools.partial(ladder_kernel, rows=rows, group=group, plane_count=plane_count),
-        grid=(count // group,),
-        in_specs=[pl.BlockSpec((group, height, LANES), lambda i: (i, 0, 0))] * rows
-        + [pl.BlockSpec(memory_space=pltpu.VMEM)]
-        + [pl.BlockSpec(acc.shape, lambda i: (0, 0))],
-        out_specs=pl.BlockSpec(acc.shape, lambda i: (0, 0)),
+        functools.partial(ladder_kernel, rows=rows, group=group, team=team, plane_count=plane_count),
+        in_specs=[vmem] * (rows + 2),
+        out_specs=vmem,
         out_shape=jax.ShapeDtypeStruct(acc.shape, jnp.float32),
         scratch_shapes=[
             pltpu.VMEM((group * WIN, width), jnp.bfloat16),
-            pltpu.VMEM((group, plane_count * WIN, BLOCK), jnp.bfloat16),
+            pltpu.VMEM((group // team, team * plane_count * WIN, width), jnp.bfloat16),
+            pltpu.VMEM((group // team, width, team * WIN), jnp.bfloat16),
         ],
-        compiler_params=pltpu.CompilerParams(vmem_limit_bytes=24 << 20),
+        compiler_params=pltpu.CompilerParams(vmem_limit_bytes=10 << 20),
         cost_estimate=pl.CostEstimate(
             flops=2 * count * plane_count * WIN * width * width,
             bytes_accessed=2 * count * width * WIN,
@@ -273,7 +283,7 @@
         in_specs=[pl.BlockSpec(memory_space=pltpu.SMEM)] * 2 + [vmem] * 2,
         out_specs=vmem,
         out_shape=jax.ShapeDtypeStruct((3, *own.shape), own.dtype),
-        compiler_params=pltpu.CompilerParams(vmem_limit_bytes=12 << 20),
+        compiler_params=pltpu.CompilerParams(vmem_limit_bytes=6 << 20),
         cost_estimate=pl.CostEstimate(flops=1 << 24, bytes_accessed=own.size * 10, transcendentals=0),
     )(row[None], tile_irrep, own, other)
 
@@ -327,7 +337,9 @@
     chunks = []
     start = 0
     for count in chunk_sizes(factors.shape[0] // row_count):
-        pieces = split_chunk(factors, row, start, count, row_count)
+        pieces = {}
+        for steps in (range(row_count - 1, 1, -1), range(1, -1, -1)):
+            pieces.update(zip(steps, split_chunk(factors, row, start, count, row_count, list(steps))))
         arrived = [pieces[0]]
         for x in range(1, row_count):
             arrived.append(lax.ppermute(pieces[x], "row", [(i, i ^ x) for i in range(row_count)]))

time: 215 us -> 216 us (level)
  waiting for transfers between devices: 81.9 us -> 96.5 us
  Pallas kernels: 80.8 us -> 66.9 us
    pallas_call x5, Pallas kernels: 63 us -> 43 us  [contract(): pl.pallas_call(functools.partial(ladder_kernel, rows=rows, group=group, t...]
    ppermute x15, waiting for transfers between devices: 58.5 us -> 73.1 us  [per_device(): lax.ppermute(pieces[x], 'row', [(i, i ^ x) for i in range(row_count)])]
    pallas_call x5 -> x10, Pallas kernels: 12.5 us -> 18.5 us  [split_chunk(): pl.pallas_call(split_kernel, grid_spec=pltpu.PrefetchScalarGridSpec(num_s...]
  transfers between devices with their start and end apart: 30 -> 30, of which waited for: 14 -> 16; matrix products, arithmetic and copies ran while one was open for 0% -> 0% of each run, Pallas kernels for 35% -> 29%
where the time goes in v1:
time: 216 us; the launch traced here: 215 us
  waiting for transfers between devices  96.5 us (45%)
  Pallas kernels  66.9 us (31%)
  starting transfers between devices  24.8 us (11%)
  blocking collectives  21.4 us (10%)
  local copies, waits for them, and re-layouts  4.71 us (2%)
    ppermute x15, waiting for transfers between devices, per_device(): lax.ppermute(pieces[x], 'row', [(i, i ^ x) for i in range(row_count)])  73.1 us
    pallas_call x5, Pallas kernels, contract(): pl.pallas_call(functools.partial(ladder_kernel, rows=rows, group=group, t...  43 us
    ppermute x7, waiting for transfers between devices, ring_gather(): up = lax.ppermute(up, axis, ahead)  21.3 us
    pallas_call x10, Pallas kernels, split_chunk(): pl.pallas_call(split_kernel, grid_spec=pltpu.PrefetchScalarGridSpec(num_s...  18.5 us
    all_to_all x1, blocking collectives, per_device(): summed = lax.all_to_all(blocks, ('row', 'col'), 0, 0, tiled=True).sum(0)  11.3 us
    ppermute x7, starting transfers between devices, ring_gather(): up = lax.ppermute(up, axis, ahead)  11.1 us
    ppermute x15, starting transfers between devices, per_device(): lax.ppermute(pieces[x], 'row', [(i, i ^ x) for i in range(row_count)])  10.2 us
    all_to_all x1, blocking collectives, amplitude_planes(): mine = lax.all_to_all(to_send, 'row', 0, 0)  10 us
  transfers between devices with their start and end apart: 30, of which 16 were waited for; matrix products, arithmetic and copies ran while one was open for 0% of the time, Pallas kernels for 29%

profile of v1, /device:TPU:0, one launch (start us, length us, event | category | flops | bytes accessed | tf_op | source)
XLA Modules:
  0.0 215.0 jit_solution(8856652309654929013)
XLA Ops:
  3.6 10.0 %all_to_all.15 = bf16[4,256,128]{2,1,0:T(8,128)(2,1)S(1)} all-to-all(bf16[4,256,128]{2,1,0:T(8,128)(2,1)S(1)} %shard_map.48), channel_id=1, replica_groups=mesh['row'=4,'col'=8] {'row'}, dimensions={0} | all-to-all | bytes 524288 | tf_op jit(solution)/shard_map/all_to_all | solution.py:325
  13.6 1.6 collective-permute-start.3
  16.1 2.6 %collective-permute-done.3 = bf16[512,128]{1,0:T(8,128)(2,1)S(1)} collective-permute-done((bf16[512,128]{1,0:T(8,128)(2,1)S(1)}, bf16[512,128]{1,0:T(8,128)(2,1)S(1)}, u32[]{:S(2)}, u32[]{:S(2)}) %collective-permute-start.3) | collective-permute-done | bytes 131104 | tf_op jit(solution)/shard_map/ppermute | solution.py:174
  18.7 1.6 collective-permute-start.5
  20.8 3.1 %collective-permute-done.5 = bf16[512,128]{1,0:T(8,128)(2,1)S(1)} collective-permute-done((bf16[512,128]{1,0:T(8,128)(2,1)S(1)}, bf16[512,128]{1,0:T(8,128)(2,1)S(1)}, u32[]{:S(2)}, u32[]{:S(2)}) %collective-permute-start.5) | collective-permute-done | bytes 131104 | tf_op jit(solution)/shard_map/ppermute | solution.py:174
  26.0 3.9 %collective-permute-done.7 = bf16[512,128]{1,0:T(8,128)(2,1)S(1)} collective-permute-done((bf16[512,128]{1,0:T(8,128)(2,1)S(1)}, bf16[512,128]{1,0:T(8,128)(2,1)S(1)}, u32[]{:S(2)}, u32[]{:S(2)}) %collective-permute-start.7) | collective-permute-done | bytes 131104 | tf_op jit(solution)/shard_map/ppermute | solution.py:174
  29.9 1.6 collective-permute-start.9
  32.3 3.4 %collective-permute-done.9 = bf16[512,128]{1,0:T(8,128)(2,1)S(1)} collective-permute-done((bf16[512,128]{1,0:T(8,128)(2,1)S(1)}, bf16[512,128]{1,0:T(8,128)(2,1)S(1)}, u32[]{:S(2)}, u32[]{:S(2)}) %collective-permute-start.9) | collective-permute-done | bytes 131104 | tf_op jit(solution)/shard_map/ppermute | solution.py:174
  35.8 1.6 collective-permute-start.11
  37.9 2.9 %collective-permute-done.11 = bf16[512,128]{1,0:T(8,128)(2,1)S(1)} collective-permute-done((bf16[512,128]{1,0:T(8,128)(2,1)S(1)}, bf16[512,128]{1,0:T(8,128)(2,1)S(1)}, u32[]{:S(2)}, u32[]{:S(2)}) %collective-permute-start.11) | collective-permute-done | bytes 131104 | tf_op jit(solution)/shard_map/ppermute | solution.py:174
  40.7 1.6 collective-permute-start.13
  42.9 2.8 %collective-permute-done.13 = bf16[512,128]{1,0:T(8,128)(2,1)S(1)} collective-permute-done((bf16[512,128]{1,0:T(8,128)(2,1)S(1)}, bf16[512,128]{1,0:T(8,128)(2,1)S(1)}, u32[]{:S(2)}, u32[]{:S(2)}) %collective-permute-start.13) | collective-permute-done | bytes 131104 | tf_op jit(solution)/shard_map/ppermute | solution.py:174
  45.7 1.6 collective-permute-start.15
  48.1 2.6 %collective-permute-done.15 = bf16[512,128]{1,0:T(8,128)(2,1)S(1)} collective-permute-done((bf16[512,128]{1,0:T(8,128)(2,1)S(1)}, bf16[512,128]{1,0:T(8,128)(2,1)S(1)}, u32[]{:S(2)}, u32[]{:S(2)}) %collective-permute-start.15) | collective-permute-done | bytes 131104 | tf_op jit(solution)/shard_map/ppermute | solution.py:174
  50.7 1.8 collective-permute-done.16
  52.7 2.7 %shard_map.54 = (bf16[32,128,128]{2,1,0:T(8,128)(2,1)S(1)}, bf16[32,128,128]{2,1,0:T(8,128)(2,1)S(1)}) custom-call(s32[1]{0:T(128)} %bitcast.row_ref, bf16[384,16384]{1,0:T(8,128)(2,1)} %refs_1_.19, bf16[384,16384]{1,0:T(8,128)(2,1)} %refs_1_.19), custom_call_target="tpu_custom_call" | custom-call | bytes 4194304 | tf_op jit(solution)/shard_map/pallas_call | solution.py:71
  55.9 2.7 %shard_map.55 = (bf16[32,128,128]{2,1,0:T(8,128)(2,1)S(1)}, bf16[32,128,128]{2,1,0:T(8,128)(2,1)S(1)}) custom-call(s32[1]{0:T(128)} %bitcast.row_ref, bf16[384,16384]{1,0:T(8,128)(2,1)} %refs_1_.19, bf16[384,16384]{1,0:T(8,128)(2,1)} %refs_1_.19), custom_call_target="tpu_custom_call" | custom-call | bytes 4194304 | tf_op jit(solution)/shard_map/pallas_call | solution.py:71
  65.0 2.7 %shard_map.52 = (bf16[32,128,128]{2,1,0:T(8,128)(2,1)S(1)}, bf16[32,128,128]{2,1,0:T(8,128)(2,1)S(1)}) custom-call(s32[1]{0:T(128)} %bitcast.row_ref, bf16[384,16384]{1,0:T(8,128)(2,1)} %refs_1_.19, bf16[384,16384]{1,0:T(8,128)(2,1)} %refs_1_.19), custom_call_target="tpu_custom_call" | custom-call | bytes 4194304 | tf_op jit(solution)/shard_map/pallas_call | solution.py:71
  67.7 2.7 %shard_map.53 = (bf16[32,128,128]{2,1,0:T(8,128)(2,1)S(1)}, bf16[32,128,128]{2,1,0:T(8,128)(2,1)S(1)}) custom-call(s32[1]{0:T(128)} %bitcast.row_ref, bf16[384,16384]{1,0:T(8,128)(2,1)} %refs_1_.19, bf16[384,16384]{1,0:T(8,128)(2,1)} %refs_1_.19), custom_call_target="tpu_custom_call" | custom-call | bytes 4194304 | tf_op jit(solution)/shard_map/pallas_call | solution.py:71
  75.8 4.2 %shard_map.49.refs_4_ = bf16[3,1024,1024]{2,1,0:T(8,128)(2,1)S(1)} custom-call(s32[1]{0:T(128)} %bitcast.row_ref, s32[16]{0:T(128)S(1)} %copy-done.3, bf16[1024,1024]{1,0:T(8,128)(2,1)S(1)} %constant_dynamic-update-slice_fusion.own_ref, bf16[1024,1024]{1,0:T(8,128)(2,1)S(1)} %collective-permute-done.17.other_ref), custom_call_target="tpu_custom_call" | custom-call | flops 16777216 | bytes 10485760 | tf_op jit(solution)/shard_map/pallas_call | solution.py:281
  80.0 32.8 %collective-permute-done.28.refs_2_ = bf16[8,128,128]{2,1,0:T(8,128)(2,1)S(1)} collective-permute-done((bf16[8,128,128]{2,1,0:T(8,128)(2,1)S(1)}, bf16[8,128,128]{2,1,0:T(8,128)(2,1)S(1)}, u32[]{:S(2)}, u32[]{:S(2)}) %collective-permute-start.28) | collective-permute-done | bytes 262176 | tf_op jit(solution)/shard_map/ppermute | solution.py:345
  112.8 3.7 %collective-permute-done.29.refs_3_ = bf16[8,128,128]{2,1,0:T(8,128)(2,1)S(1)} collective-permute-done((bf16[8,128,128]{2,1,0:T(8,128)(2,1)S(1)}, bf16[8,128,128]{2,1,0:T(8,128)(2,1)S(1)}, u32[]{:S(2)}, u32[]{:S(2)}) %collective-permute-start.29) | collective-permute-done | bytes 262176 | tf_op jit(solution)/shard_map/ppermute | solution.py:345
  117.5 3.6 %shard_map.58.refs_5_ = f32[192,128]{1,0:T(8,128)S(1)} custom-call(bf16[8,128,128]{2,1,0:T(8,128)(2,1)S(1)} %get-tuple-element.41.refs_0_, bf16[8,128,128]{2,1,0:T(8,128)(2,1)S(1)} %collective-permute-done.27.refs_1_, bf16[8,128,128]{2,1,0:T(8,128)(2,1)S(1)} %collective-permute-done.28.refs_2_, bf16[8,128,128]{2,1,0:T(8,128)(2,1)S(1)} %collective-permute-done.29.refs_3_, ...), custom_call_target="tpu_custom_call" | custom-call | flops 3221225472 | bytes 1048576 | tf_op jit(solution)/shard_map/pallas_call | solution.py:137
  123.4 14.4 %shard_map.59.refs_5_ = f32[192,128]{1,0:T(8,128)S(1)} custom-call(bf16[32,128,128]{2,1,0:T(8,128)(2,1)S(1)} %get-tuple-element.37.refs_0_, bf16[32,128,128]{2,1,0:T(8,128)(2,1)S(1)} %collective-permute-done.24.refs_1_, bf16[32,128,128]{2,1,0:T(8,128)(2,1)S(1)} %collective-permute-done.25.refs_2_, bf16[32,128,128]{2,1,0:T(8,128)(2,1)S(1)} %collective-permute-done.26.refs_3_, ...), custom_call_target="tpu_custom_call" | custom-call | flops 12884901888 | bytes 4194304 | tf_op jit(solution)/shard_map/pallas_call | solution.py:137
  138.7 3.9 %collective-permute-done.22.refs_2_ = bf16[32,128,128]{2,1,0:T(8,128)(2,1)S(1)} collective-permute-done((bf16[32,128,128]{2,1,0:T(8,128)(2,1)S(1)}, bf16[32,128,128]{2,1,0:T(8,128)(2,1)S(1)}, u32[]{:S(2)}, u32[]{:S(2)}) %collective-permute-start.22) | collective-permute-done | bytes 1048608 | tf_op jit(solution)/shard_map/ppermute | solution.py:345
  142.6 22.0 %collective-permute-done.23.refs_3_ = bf16[32,128,128]{2,1,0:T(8,128)(2,1)S(1)} collective-permute-done((bf16[32,128,128]{2,1,0:T(8,128)(2,1)S(1)}, bf16[32,128,128]{2,1,0:T(8,128)(2,1)S(1)}, u32[]{:S(2)}, u32[]{:S(2)}) %collective-permute-start.23) | collective-permute-done | bytes 1048608 | tf_op jit(solution)/shard_map/ppermute | solution.py:345
  165.6 14.3 %shard_map.60.refs_5_ = f32[192,128]{1,0:T(8,128)S(1)} custom-call(bf16[32,128,128]{2,1,0:T(8,128)(2,1)S(1)} %get-tuple-element.33.refs_0_, bf16[32,128,128]{2,1,0:T(8,128)(2,1)S(1)} %collective-permute-done.21.refs_1_, bf16[32,128,128]{2,1,0:T(8,128)(2,1)S(1)} %collective-permute-done.22.refs_2_, bf16[32,128,128]{2,1,0:T(8,128)(2,1)S(1)} %collective-permute-done.23.refs_3_, ...), custom_call_target="tpu_custom_call" | custom-call | flops 12884901888 | bytes 4194304 | tf_op jit(solution)/shard_map/pallas_call | solution.py:137
  180.6 6.5 %collective-permute-done.20.refs_3_ = bf16[16,128,128]{2,1,0:T(8,128)(2,1)S(1)} collective-permute-done((bf16[16,128,128]{2,1,0:T(8,128)(2,1)S(1)}, bf16[16,128,128]{2,1,0:T(8,128)(2,1)S(1)}, u32[]{:S(2)}, u32[]{:S(2)}) %collective-permute-start.20) | collective-permute-done | bytes 524320 | tf_op jit(solution)/shard_map/ppermute | solution.py:345
  187.1 7.2 %shard_map.61.refs_5_ = f32[192,128]{1,0:T(8,128)S(1)} custom-call(bf16[16,128,128]{2,1,0:T(8,128)(2,1)S(1)} %get-tuple-element.29.refs_0_, bf16[16,128,128]{2,1,0:T(8,128)(2,1)S(1)} %collective-permute-done.18.refs_1_, bf16[16,128,128]{2,1,0:T(8,128)(2,1)S(1)} %collective-permute-done.19.refs_2_, bf16[16,128,128]{2,1,0:T(8,128)(2,1)S(1)} %collective-permute-done.20.refs_3_, ...), custom_call_target="tpu_custom_call" | custom-call | flops 6442450944 | bytes 2097152 | tf_op jit(solution)/shard_map/pallas_call | solution.py:137
  194.3 4.0 %collective-permute-done.2.refs_3_ = bf16[8,128,128]{2,1,0:T(8,128)(2,1)S(1)} collective-permute-done((bf16[8,128,128]{2,1,0:T(8,128)(2,1)S(1)}, bf16[8,128,128]{2,1,0:T(8,128)(2,1)S(1)}, u32[]{:S(2)}, u32[]{:S(2)}) %collective-permute-start.2) | collective-permute-done | bytes 262176 | tf_op jit(solution)/shard_map/ppermute | solution.py:345
  198.3 3.6 %shard_map.62 = f32[192,128]{1,0:T(8,128)S(1)} custom-call(bf16[8,128,128]{2,1,0:T(8,128)(2,1)S(1)} %get-tuple-element.25.refs_0_, bf16[8,128,128]{2,1,0:T(8,128)(2,1)S(1)} %collective-permute-done.refs_1_, bf16[8,128,128]{2,1,0:T(8,128)(2,1)S(1)} %collective-permute-done.1.refs_2_, bf16[8,128,128]{2,1,0:T(8,128)(2,1)S(1)} %collective-permute-done.2.refs_3_, ...), custom_call_target="tpu_custom_call" | custom-call | flops 3221225472 | bytes 1048576 | tf_op jit(solution)/shard_map/pallas_call | solution.py:137
  203.0 11.3 %all_to_all.16 = f32[32,1,512]{2,1,0:T(1,128)S(1)} all-to-all(f32[32,1,512]{2,1,0:T(1,128)S(1)} %all_to_all.12), channel_id=1, replica_groups=mesh['row'=4,'col'=8] {'row','col'}, dimensions={0} | all-to-all | bytes 131072 | tf_op jit(solution)/shard_map/all_to_all | solution.py:357
  (90 shorter events, 29.6 us)
Async XLA Ops:
  0.1 0.9 copy-start
  13.6 5.0 %collective-permute-start.3 = (bf16[512,128]{1,0:T(8,128)(2,1)S(1)}, bf16[512,128]{1,0:T(8,128)(2,1)S(1)}, u32[]{:S(2)}, u32[]{:S(2)}) collective-permute-start(bf16[512,128]{1,0:T(8,128)(2,1)S(1)} %bitcast.24), channel_id=1, source_target_pairs={{0,2},{2,4},{4,6},{6,7},{7,5},{5,3},{3,1},{1,0},{8,10},{10,12},{12... | collective-permute-start | bytes 393224 | tf_op jit(solution)/shard_map/ppermute | solution.py:174
  15.3 5.0 %collective-permute-start.4 = (bf16[512,128]{1,0:T(8,128)(2,1)S(1)}, bf16[512,128]{1,0:T(8,128)(2,1)S(1)}, u32[]{:S(2)}, u32[]{:S(2)}) collective-permute-start(bf16[512,128]{1,0:T(8,128)(2,1)S(1)} %bitcast.23), channel_id=1, source_target_pairs={{2,0},{4,2},{6,4},{7,6},{5,7},{3,5},{1,3},{0,1},{10,8},{12,10},{14... | collective-permute-start | bytes 393224 | tf_op jit(solution)/shard_map/ppermute | solution.py:175
  18.7 5.2 %collective-permute-start.5 = (bf16[512,128]{1,0:T(8,128)(2,1)S(1)}, bf16[512,128]{1,0:T(8,128)(2,1)S(1)}, u32[]{:S(2)}, u32[]{:S(2)}) collective-permute-start(bf16[512,128]{1,0:T(8,128)(2,1)S(1)} %collective-permute-done.3), channel_id=1, source_target_pairs={{0,2},{2,4},{4,6},{6,7},{7,5},{5,3},{3,1},{1,0},{8,10},{10,12},{12... | collective-permute-start | bytes 393224 | tf_op jit(solution)/shard_map/ppermute | solution.py:174
  20.2 5.2 %collective-permute-start.6 = (bf16[512,128]{1,0:T(8,128)(2,1)S(1)}, bf16[512,128]{1,0:T(8,128)(2,1)S(1)}, u32[]{:S(2)}, u32[]{:S(2)}) collective-permute-start(bf16[512,128]{1,0:T(8,128)(2,1)S(1)} %collective-permute-done.4), channel_id=1, source_target_pairs={{2,0},{4,2},{6,4},{7,6},{5,7},{3,5},{1,3},{0,1},{10,8},{12,10},{14... | collective-permute-start | bytes 393224 | tf_op jit(solution)/shard_map/ppermute | solution.py:175
  23.9 6.0 %collective-permute-start.7 = (bf16[512,128]{1,0:T(8,128)(2,1)S(1)}, bf16[512,128]{1,0:T(8,128)(2,1)S(1)}, u32[]{:S(2)}, u32[]{:S(2)}) collective-permute-start(bf16[512,128]{1,0:T(8,128)(2,1)S(1)} %collective-permute-done.5), channel_id=1, source_target_pairs={{0,2},{2,4},{4,6},{6,7},{7,5},{5,3},{3,1},{1,0},{8,10},{10,12},{12... | collective-permute-start | bytes 393224 | tf_op jit(solution)/shard_map/ppermute | solution.py:174
  25.4 6.3 %collective-permute-start.8 = (bf16[512,128]{1,0:T(8,128)(2,1)S(1)}, bf16[512,128]{1,0:T(8,128)(2,1)S(1)}, u32[]{:S(2)}, u32[]{:S(2)}) collective-permute-start(bf16[512,128]{1,0:T(8,128)(2,1)S(1)} %collective-permute-done.6), channel_id=1, source_target_pairs={{2,0},{4,2},{6,4},{7,6},{5,7},{3,5},{1,3},{0,1},{10,8},{12,10},{14... | collective-permute-start | bytes 393224 | tf_op jit(solution)/shard_map/ppermute | solution.py:175
  29.9 5.8 %collective-permute-start.9 = (bf16[512,128]{1,0:T(8,128)(2,1)S(1)}, bf16[512,128]{1,0:T(8,128)(2,1)S(1)}, u32[]{:S(2)}, u32[]{:S(2)}) collective-permute-start(bf16[512,128]{1,0:T(8,128)(2,1)S(1)} %collective-permute-done.7), channel_id=1, source_target_pairs={{0,2},{2,4},{4,6},{6,7},{7,5},{5,3},{3,1},{1,0},{8,10},{10,12},{12... | collective-permute-start | bytes 393224 | tf_op jit(solution)/shard_map/ppermute | solution.py:174
  31.7 5.6 %collective-permute-start.10 = (bf16[512,128]{1,0:T(8,128)(2,1)S(1)}, bf16[512,128]{1,0:T(8,128)(2,1)S(1)}, u32[]{:S(2)}, u32[]{:S(2)}) collective-permute-start(bf16[512,128]{1,0:T(8,128)(2,1)S(1)} %collective-permute-done.8), channel_id=1, source_target_pairs={{2,0},{4,2},{6,4},{7,6},{5,7},{3,5},{1,3},{0,1},{10,8},{12,10},{14... | collective-permute-start | bytes 393224 | tf_op jit(solution)/shard_map/ppermute | solution.py:175
  35.8 5.0 %collective-permute-start.11 = (bf16[512,128]{1,0:T(8,128)(2,1)S(1)}, bf16[512,128]{1,0:T(8,128)(2,1)S(1)}, u32[]{:S(2)}, u32[]{:S(2)}) collective-permute-start(bf16[512,128]{1,0:T(8,128)(2,1)S(1)} %collective-permute-done.9), channel_id=1, source_target_pairs={{0,2},{2,4},{4,6},{6,7},{7,5},{5,3},{3,1},{1,0},{8,10},{10,12},{12... | collective-permute-start | bytes 393224 | tf_op jit(solution)/shard_map/ppermute | solution.py:174
  37.3 5.0 %collective-permute-start.12 = (bf16[512,128]{1,0:T(8,128)(2,1)S(1)}, bf16[512,128]{1,0:T(8,128)(2,1)S(1)}, u32[]{:S(2)}, u32[]{:S(2)}) collective-permute-start(bf16[512,128]{1,0:T(8,128)(2,1)S(1)} %collective-permute-done.10), channel_id=1, source_target_pairs={{2,0},{4,2},{6,4},{7,6},{5,7},{3,5},{1,3},{0,1},{10,8},{12,10},{14... | collective-permute-start | bytes 393224 | tf_op jit(solution)/shard_map/ppermute | solution.py:175
  40.7 5.0 %collective-permute-start.13 = (bf16[512,128]{1,0:T(8,128)(2,1)S(1)}, bf16[512,128]{1,0:T(8,128)(2,1)S(1)}, u32[]{:S(2)}, u32[]{:S(2)}) collective-permute-start(bf16[512,128]{1,0:T(8,128)(2,1)S(1)} %collective-permute-done.11), channel_id=1, source_target_pairs={{0,2},{2,4},{4,6},{6,7},{7,5},{5,3},{3,1},{1,0},{8,10},{10,12},{12... | collective-permute-start | bytes 393224 | tf_op jit(solution)/shard_map/ppermute | solution.py:174
  42.4 5.0 %collective-permute-start.14 = (bf16[512,128]{1,0:T(8,128)(2,1)S(1)}, bf16[512,128]{1,0:T(8,128)(2,1)S(1)}, u32[]{:S(2)}, u32[]{:S(2)}) collective-permute-start(bf16[512,128]{1,0:T(8,128)(2,1)S(1)} %collective-permute-done.12), channel_id=1, source_target_pairs={{2,0},{4,2},{6,4},{7,6},{5,7},{3,5},{1,3},{0,1},{10,8},{12,10},{14... | collective-permute-start | bytes 393224 | tf_op jit(solution)/shard_map/ppermute | solution.py:175
  45.7 5.0 %collective-permute-start.15 = (bf16[512,128]{1,0:T(8,128)(2,1)S(1)}, bf16[512,128]{1,0:T(8,128)(2,1)S(1)}, u32[]{:S(2)}, u32[]{:S(2)}) collective-permute-start(bf16[512,128]{1,0:T(8,128)(2,1)S(1)} %collective-permute-done.13), channel_id=1, source_target_pairs={{0,2},{2,4},{4,6},{6,7},{7,5},{5,3},{3,1},{1,0},{8,10},{10,12},{12... | collective-permute-start | bytes 393224 | tf_op jit(solution)/shard_map/ppermute | solution.py:174
  47.4 5.1 %collective-permute-start.16 = (bf16[512,128]{1,0:T(8,128)(2,1)S(1)}, bf16[512,128]{1,0:T(8,128)(2,1)S(1)}, u32[]{:S(2)}, u32[]{:S(2)}) collective-permute-start(bf16[512,128]{1,0:T(8,128)(2,1)S(1)} %collective-permute-done.14), channel_id=1, source_target_pairs={{2,0},{4,2},{6,4},{7,6},{5,7},{3,5},{1,3},{0,1},{10,8},{12,10},{14... | collective-permute-start | bytes 393224 | tf_op jit(solution)/shard_map/ppermute | solution.py:175
  52.6 11.8 %collective-permute-start.17 = (bf16[1024,1024]{1,0:T(8,128)(2,1)S(1)}, bf16[1024,1024]{1,0:T(8,128)(2,1)S(1)}, u32[]{:S(2)}, u32[]{:S(2)}) collective-permute-start(bf16[1024,1024]{1,0:T(8,128)(2,1)S(1)} %constant_dynamic-update-slice_fusion.own_ref), channel_id=1, source_target_pairs={{0,8},{8,0},{16,24},{24,16},{1,9},{9,1},{17,25},{25,17},{2,10},{10... | collective-permute-start | bytes 6291464 | tf_op jit(solution)/shard_map/ppermute | solution.py:327
  55.4 65.8 %collective-permute-start.24 = (bf16[32,128,128]{2,1,0:T(8,128)(2,1)S(1)}, bf16[32,128,128]{2,1,0:T(8,128)(2,1)S(1)}, u32[]{:S(2)}, u32[]{:S(2)}) collective-permute-start(bf16[32,128,128]{2,1,0:T(8,128)(2,1)S(1)} %get-tuple-element.38), channel_id=1, source_target_pairs={{0,8},{8,0},{16,24},{24,16},{1,9},{9,1},{17,25},{25,17},{2,10},{10... | collective-permute-start | bytes 3145736 | tf_op jit(solution)/shard_map/ppermute | solution.py:345
  58.6 63.7 %collective-permute-start.25 = (bf16[32,128,128]{2,1,0:T(8,128)(2,1)S(1)}, bf16[32,128,128]{2,1,0:T(8,128)(2,1)S(1)}, u32[]{:S(2)}, u32[]{:S(2)}) collective-permute-start(bf16[32,128,128]{2,1,0:T(8,128)(2,1)S(1)} %get-tuple-element.39), channel_id=1, source_target_pairs={{0,16},{8,24},{16,0},{24,8},{1,17},{9,25},{17,1},{25,9},{2,18},{10... | collective-permute-start | bytes 3145736 | tf_op jit(solution)/shard_map/ppermute | solution.py:345
  59.6 62.7 %collective-permute-start.26 = (bf16[32,128,128]{2,1,0:T(8,128)(2,1)S(1)}, bf16[32,128,128]{2,1,0:T(8,128)(2,1)S(1)}, u32[]{:S(2)}, u32[]{:S(2)}) collective-permute-start(bf16[32,128,128]{2,1,0:T(8,128)(2,1)S(1)} %get-tuple-element.40), channel_id=1, source_target_pairs={{0,24},{8,16},{16,8},{24,0},{1,25},{9,17},{17,9},{25,1},{2,26},{10... | collective-permute-start | bytes 3145736 | tf_op jit(solution)/shard_map/ppermute | solution.py:345
  61.3 2.0 collective-permute-start.27
  63.3 49.5 %collective-permute-start.28 = (bf16[8,128,128]{2,1,0:T(8,128)(2,1)S(1)}, bf16[8,128,128]{2,1,0:T(8,128)(2,1)S(1)}, u32[]{:S(2)}, u32[]{:S(2)}) collective-permute-start(bf16[8,128,128]{2,1,0:T(8,128)(2,1)S(1)} %get-tuple-element.43), channel_id=1, source_target_pairs={{0,16},{8,24},{16,0},{24,8},{1,17},{9,25},{17,1},{25,9},{2,18},{10... | collective-permute-start | bytes 786440 | tf_op jit(solution)/shard_map/ppermute | solution.py:345
  64.4 52.2 %collective-permute-start.29 = (bf16[8,128,128]{2,1,0:T(8,128)(2,1)S(1)}, bf16[8,128,128]{2,1,0:T(8,128)(2,1)S(1)}, u32[]{:S(2)}, u32[]{:S(2)}) collective-permute-start(bf16[8,128,128]{2,1,0:T(8,128)(2,1)S(1)} %get-tuple-element.44), channel_id=1, source_target_pairs={{0,24},{8,16},{16,8},{24,0},{1,25},{9,17},{17,9},{25,1},{2,26},{10... | collective-permute-start | bytes 786440 | tf_op jit(solution)/shard_map/ppermute | solution.py:345
  74.5 1.2 copy-start.3
  112.8 25.0 %collective-permute-start.21 = (bf16[32,128,128]{2,1,0:T(8,128)(2,1)S(1)}, bf16[32,128,128]{2,1,0:T(8,128)(2,1)S(1)}, u32[]{:S(2)}, u32[]{:S(2)}) collective-permute-start(bf16[32,128,128]{2,1,0:T(8,128)(2,1)S(1)} %get-tuple-element.34), channel_id=1, source_target_pairs={{0,8},{8,0},{16,24},{24,16},{1,9},{9,1},{17,25},{25,17},{2,10},{10... | collective-permute-start | bytes 3145736 | tf_op jit(solution)/shard_map/ppermute | solution.py:345
  116.5 26.0 %collective-permute-start.22 = (bf16[32,128,128]{2,1,0:T(8,128)(2,1)S(1)}, bf16[32,128,128]{2,1,0:T(8,128)(2,1)S(1)}, u32[]{:S(2)}, u32[]{:S(2)}) collective-permute-start(bf16[32,128,128]{2,1,0:T(8,128)(2,1)S(1)} %get-tuple-element.35), channel_id=1, source_target_pairs={{0,16},{8,24},{16,0},{24,8},{1,17},{9,25},{17,1},{25,9},{2,18},{10... | collective-permute-start | bytes 3145736 | tf_op jit(solution)/shard_map/ppermute | solution.py:345
  121.1 43.5 %collective-permute-start.23 = (bf16[32,128,128]{2,1,0:T(8,128)(2,1)S(1)}, bf16[32,128,128]{2,1,0:T(8,128)(2,1)S(1)}, u32[]{:S(2)}, u32[]{:S(2)}) collective-permute-start(bf16[32,128,128]{2,1,0:T(8,128)(2,1)S(1)} %get-tuple-element.36), channel_id=1, source_target_pairs={{0,24},{8,16},{16,8},{24,0},{1,25},{9,17},{17,9},{25,1},{2,26},{10... | collective-permute-start | bytes 3145736 | tf_op jit(solution)/shard_map/ppermute | solution.py:345
  122.3 57.5 %collective-permute-start.18 = (bf16[16,128,128]{2,1,0:T(8,128)(2,1)S(1)}, bf16[16,128,128]{2,1,0:T(8,128)(2,1)S(1)}, u32[]{:S(2)}, u32[]{:S(2)}) collective-permute-start(bf16[16,128,128]{2,1,0:T(8,128)(2,1)S(1)} %get-tuple-element.30), channel_id=1, source_target_pairs={{0,8},{8,0},{16,24},{24,16},{1,9},{9,1},{17,25},{25,17},{2,10},{10... | collective-permute-start | bytes 1572872 | tf_op jit(solution)/shard_map/ppermute | solution.py:345
  122.4 58.2 %collective-permute-start.19 = (bf16[16,128,128]{2,1,0:T(8,128)(2,1)S(1)}, bf16[16,128,128]{2,1,0:T(8,128)(2,1)S(1)}, u32[]{:S(2)}, u32[]{:S(2)}) collective-permute-start(bf16[16,128,128]{2,1,0:T(8,128)(2,1)S(1)} %get-tuple-element.31), channel_id=1, source_target_pairs={{0,16},{8,24},{16,0},{24,8},{1,17},{9,25},{17,1},{25,9},{2,18},{10... | collective-permute-start | bytes 1572872 | tf_op jit(solution)/shard_map/ppermute | solution.py:345
  137.8 49.3 %collective-permute-start.20 = (bf16[16,128,128]{2,1,0:T(8,128)(2,1)S(1)}, bf16[16,128,128]{2,1,0:T(8,128)(2,1)S(1)}, u32[]{:S(2)}, u32[]{:S(2)}) collective-permute-start(bf16[16,128,128]{2,1,0:T(8,128)(2,1)S(1)} %get-tuple-element.32), channel_id=1, source_target_pairs={{0,24},{8,16},{16,8},{24,0},{1,25},{9,17},{17,9},{25,1},{2,26},{10... | collective-permute-start | bytes 1572872 | tf_op jit(solution)/shard_map/ppermute | solution.py:345
  142.6 51.7 %collective-permute-start = (bf16[8,128,128]{2,1,0:T(8,128)(2,1)S(1)}, bf16[8,128,128]{2,1,0:T(8,128)(2,1)S(1)}, u32[]{:S(2)}, u32[]{:S(2)}) collective-permute-start(bf16[8,128,128]{2,1,0:T(8,128)(2,1)S(1)} %get-tuple-element.26), channel_id=1, source_target_pairs={{0,8},{8,0},{16,24},{24,16},{1,9},{9,1},{17,25},{25,17},{2,10},{10... | collective-permute-start | bytes 786440 | tf_op jit(solution)/shard_map/ppermute | solution.py:345
  164.6 29.7 %collective-permute-start.1 = (bf16[8,128,128]{2,1,0:T(8,128)(2,1)S(1)}, bf16[8,128,128]{2,1,0:T(8,128)(2,1)S(1)}, u32[]{:S(2)}, u32[]{:S(2)}) collective-permute-start(bf16[8,128,128]{2,1,0:T(8,128)(2,1)S(1)} %get-tuple-element.27), channel_id=1, source_target_pairs={{0,16},{8,24},{16,0},{24,8},{1,17},{9,25},{17,1},{25,9},{2,18},{10... | collective-permute-start | bytes 786440 | tf_op jit(solution)/shard_map/ppermute | solution.py:345
  179.9 18.4 %collective-permute-start.2 = (bf16[8,128,128]{2,1,0:T(8,128)(2,1)S(1)}, bf16[8,128,128]{2,1,0:T(8,128)(2,1)S(1)}, u32[]{:S(2)}, u32[]{:S(2)}) collective-permute-start(bf16[8,128,128]{2,1,0:T(8,128)(2,1)S(1)} %get-tuple-element.28), channel_id=1, source_target_pairs={{0,24},{8,16},{16,8},{24,0},{1,25},{9,17},{17,9},{25,1},{2,26},{10... | collective-permute-start | bytes 786440 | tf_op jit(solution)/shard_map/ppermute | solution.py:345
  (2 other events, 1.4 us)
